TPU v7x, 512 devices: a whole 4x4x16 slice. The times are simulated.
512 devices in a mesh: group: 16 (over x, y), dev: 32 (over z, core).
Axes of the slice: x: 4, y: 4, z: 16, core: 2. Of those that a mesh axis runs over, the one named last changes fastest.
Arguments:
- embeddings: bfloat16 [655360, 768], P(('group', 'dev')), may hold values from -6 to 6
- projection: bfloat16 [256, 768], replicated, may hold values from -0.21875 to 0.21875
- triplets: int32 [3, 1048576], P(None, ('group', 'dev')), may hold values from 0 to 3327, as said below
- cotangent: float32 [1048576], P(('group', 'dev')), may hold values from -24 to 24
- wanted_rows: int32 [8192, 128], P(('group', 'dev')), may hold values from -1 to 1279, as said below
Outputs:
- row_grad: bfloat16 [655360, 768], P(('group', 'dev'))
- weight_grad: float32 [256, 768], replicated
Inputs may be any that keep to these rules, and one draw needn't show every extreme that they name: `wanted_rows`: in each list the live entries come first and are distinct rows of the owning device, the rest are -1; each list holds from 128 // 4 (at least 1) to 128 live entries; all lists of some group of requesters are full, and all lists sent to some group are full. `triplets`: anchors are below 1280; a positive or negative below 1280 is one of the device's own rows, else 1280 + h * 128 + s names a live slot s of the device's list for group h.
All inputs are finite; a program needn't handle non-finite values.
Results may differ from a plain program's by a relative error of at most 0.0058.
Values may be sent and summed in bfloat16 or wider, within the bound.
No kernel may reach another device: no remote copies, remote signals or barrier semaphores. Data moves between devices by JAX's collectives and lax.ppermute only.
A program may use at most 64 MiB of HBM per device.

v0:
```python
import math
import jax
import jax.numpy as jnp
from jax import lax
from jax.sharding import PartitionSpec as P

distance_scale = 0.0625
margin = 1.0
pull_share = 0.5


def triplet_gradients(lookup, triple, cotangent):
    anchor_rows = lookup[triple[0]].astype(jnp.float32)
    positive_rows = lookup[triple[1]].astype(jnp.float32)
    negative_rows = lookup[triple[2]].astype(jnp.float32)
    to_positive = anchor_rows - positive_rows
    to_negative = anchor_rows - negative_rows
    near = distance_scale * jnp.sum(to_positive * to_positive, axis=1)
    far = distance_scale * jnp.sum(to_negative * to_negative, axis=1)
    hinge_gate = jax.nn.sigmoid(margin + near - far)
    pull_factor = 2.0 * distance_scale * cotangent * (1.0 - pull_share + pull_share * hinge_gate)
    push_factor = 2.0 * distance_scale * cotangent * pull_share * hinge_gate
    pull_term = pull_factor[:, None] * to_positive
    push_term = push_factor[:, None] * to_negative
    gradient = jnp.zeros(lookup.shape, jnp.float32)
    gradient = gradient.at[triple[0]].add(pull_term - push_term)
    gradient = gradient.at[triple[1]].add(-pull_term)
    gradient = gradient.at[triple[2]].add(push_term)
    return gradient


def local(embeddings, projection, triplets, cotangent, wanted_rows):
    shard_rows = embeddings.shape[0]
    rank_width = projection.shape[0]
    groups = lax.axis_size("group")
    contract = (((1,), (1,)), ((), ()))
    own_projected = lax.dot_general(
        embeddings, projection, contract, preferred_element_type=jnp.float32
    ).astype(jnp.bfloat16)
    wanted = lax.all_to_all(wanted_rows, "group", split_axis=0, concat_axis=0, tiled=True)
    served_index = jnp.maximum(wanted, 0)
    served = own_projected[served_index]
    fetched = lax.all_to_all(served, "group", split_axis=0, concat_axis=0, tiled=True)
    lookup = jnp.concatenate([own_projected, fetched.reshape(-1, rank_width)], axis=0)
    gradient = triplet_gradients(lookup, triplets, cotangent)
    remote_grad = gradient[shard_rows:].reshape(groups, -1, rank_width).astype(jnp.bfloat16)
    returned = lax.all_to_all(remote_grad, "group", split_axis=0, concat_axis=0, tiled=True)
    row_total = (
        gradient[:shard_rows]
        .at[served_index.reshape(-1)]
        .add(returned.reshape(-1, rank_width).astype(jnp.float32))
    )
    row_rounded = row_total.astype(jnp.bfloat16)
    row_grad = jnp.dot(row_rounded, projection, preferred_element_type=jnp.float32).astype(
        jnp.bfloat16
    )
    partial_value = lax.dot_general(
        row_rounded, embeddings, (((0,), (0,)), ((), ())), preferred_element_type=jnp.float32
    )
    factor = 1.0 / math.sqrt(cotangent.shape[0] * groups * lax.axis_size("dev"))
    weight_total = lax.psum(partial_value, ("group", "dev"))
    return (row_grad, weight_total * factor)


def solution(mesh):
    return jax.shard_map(
        local,
        mesh=mesh,
        in_specs=(
            P(("group", "dev"), None),
            P(),
            P(None, ("group", "dev")),
            P(("group", "dev")),
            P(("group", "dev"), None),
        ),
        out_specs=(P(("group", "dev"), None), P()),
        check_vma=False,
    )
```

profile of v0, /device:TPU:2, one launch (start us, length us, event | category | flops | bytes accessed | tf_op | source)
XLA Modules:
  0.0 648.8 jit_solution(12373123322807966387)
XLA Ops:
  7.2 0.0 copy-start
  7.2 9.3 %all-to-all-start = ((s32[16,1,128]{2,1,0:T(1,128)}), s32[16,1,128]{2,1,0:T(1,128)S(1)}, u32[]{:S(2)}, u32[]{:S(2)}) async-start(s32[16,1,128]{2,1,0:T(1,128)} %bitcast.29), calls=%async_computation | async-start | bytes 16384 | tf_op jit(solution)/shard_map/all_to_all | solution.py:40
  16.5 0.0 copy-done
  16.5 1.7 convolution_convert_fusion.1
  18.2 4.5 all-to-all-done
  22.7 9.1 %gather_fusion = bf16[2048,256]{1,0:T(8,128)(2,1)} fusion(bf16[1280,256]{1,0:T(8,128)(2,1)S(1)} %convolution_convert_fusion.1, s32[2048]{0:T(1024)S(1)} %broadcast_clamp_fusion.3), kind=kCustom, calls=%fused_computation | custom fusion | bytes 2105344 | tf_op jit(solution)/shard_map/gather | solution.py:42
  31.8 0.0 copy-start.1
  31.8 5.7 all-to-all-start.1
  37.4 0.0 copy-done.1
  37.5 12.2 %all-to-all-done.1 = bf16[16,128,256]{2,1,0:T(8,128)(2,1)} async-done(((bf16[16,128,256]{2,1,0:T(8,128)(2,1)}), bf16[16,128,256]{2,1,0:T(8,128)(2,1)}, u32[]{:S(2)}, u32[]{:S(2)}) %all-to-all-start.1) | async-done | bytes 1048608 | tf_op jit(solution)/shard_map/all_to_all | solution.py:43
  49.7 2.5 pad_maximum_fusion
  52.2 8.3 %gather_fusion.1 = bf16[2048,256]{1,0:T(8,128)(2,1)S(1)} fusion(bf16[3328,256]{1,0:T(8,128)(2,1)} %pad_maximum_fusion, s32[2048]{0:T(1024)S(1)} %broadcast_clamp_fusion.2), kind=kCustom, calls=%fused_computation.1 | custom fusion | bytes 2105344 | tf_op jit(solution)/shard_map/gather | solution.py:13
  60.5 10.1 %gather_fusion.3 = bf16[2048,256]{1,0:T(8,128)(2,1)} fusion(bf16[3328,256]{1,0:T(8,128)(2,1)} %pad_maximum_fusion, s32[2048]{0:T(1024)S(1)} %broadcast_clamp_fusion), kind=kCustom, calls=%fused_computation.3 | custom fusion | bytes 2105344 | tf_op jit(solution)/shard_map/gather | solution.py:15
  70.7 10.1 %gather_fusion.2 = bf16[2048,256]{1,0:T(8,128)(2,1)} fusion(bf16[3328,256]{1,0:T(8,128)(2,1)} %pad_maximum_fusion, s32[2048]{0:T(1024)S(1)} %broadcast_clamp_fusion.1), kind=kCustom, calls=%fused_computation.2 | custom fusion | bytes 2105344 | tf_op jit(solution)/shard_map/gather | solution.py:14
  80.8 0.0 copy-start.2
  80.8 2.5 multiply_reduce_fusion.1
  83.3 0.0 copy-done.2
  83.3 15.1 %scatter_custom_fusion = f32[3328,256]{1,0:T(8,128)} fusion(s32[2048]{0:T(1024)S(1)} %bitcast.28, bf16[2048,256]{1,0:T(8,128)(2,1)} %gather_fusion.3, bf16[2048,256]{1,0:T(8,128)(2,1)S(1)} %gather_fusion.1, bf16[2048,256]{1,0:T(8,128)(2,1)} %gather_fusion.2, f32[]{:T(128)} %constant.8.clone.1, f32[2048]{0:T(1024)S(1)} %get-tuple-element.8, ...), kind=kCustom, calls=%fused_computation.17 | custom fusion | flops 4718592 | bytes 6569988 | tf_op jit(solution)/shard_map/scatter-add | solution.py:26
  98.4 16.7 %scatter_custom_fusion.1 = f32[3328,256]{1,0:T(8,128)} fusion(f32[3328,256]{1,0:T(8,128)} %scatter_custom_fusion, s32[2048]{0:T(1024)S(1)} %bitcast.26, bf16[2048,256]{1,0:T(8,128)(2,1)} %gather_fusion.2, bf16[2048,256]{1,0:T(8,128)(2,1)S(1)} %gather_fusion.1, f32[2048]{0:T(1024)S(1)} %get-tuple-element.7), kind=kCustom, calls=%fused_computation.15 | custom fusion | flops 3145728 | bytes 5513216 | tf_op jit(solution)/shard_map/scatter-add | solution.py:27
  115.1 16.6 %scatter_custom_fusion.2 = f32[3328,256]{1,0:T(8,128)} fusion(f32[3328,256]{1,0:T(8,128)} %scatter_custom_fusion.1, s32[2048]{0:T(1024)S(1)} %bitcast.24, bf16[2048,256]{1,0:T(8,128)(2,1)} %gather_fusion.3, bf16[2048,256]{1,0:T(8,128)(2,1)S(1)} %gather_fusion.1, f32[2048]{0:T(1024)S(1)} %get-tuple-element.8), kind=kCustom, calls=%fused_computation.23 | custom fusion | flops 2621440 | bytes 5513216 | tf_op jit(solution)/shard_map/scatter-add | solution.py:28
  131.7 2.7 slice.38
  134.4 6.3 all-to-all-start.2
  140.7 0.0 all-reduce.2.cloned.1.call-start
  140.8 1.4 slice.32
  142.2 9.6 %all-to-all-done.2 = bf16[16,128,256]{2,1,0:T(8,128)(2,1)} async-done(((bf16[16,128,256]{2,1,0:T(8,128)(2,1)}), bf16[16,128,256]{2,1,0:T(8,128)(2,1)}, u32[]{:S(2)}, u32[]{:S(2)}) %all-to-all-start.2) | async-done | bytes 1048608 | tf_op jit(solution)/shard_map/all_to_all | solution.py:47
  151.7 13.6 %scatter_custom_fusion.3 = f32[1280,256]{1,0:T(8,128)S(1)} fusion(f32[1280,256]{1,0:T(8,128)S(1)} %slice.32, s32[2048]{0:T(1024)S(1)} %bitcast.22, bf16[2048,256]{1,0:T(8,128)(2,1)} %bitcast.12), kind=kCustom, calls=%fused_computation.13 | custom fusion | flops 1048576 | bytes 2359296 | tf_op jit(solution)/shard_map/scatter-add | solution.py:51
  165.3 1.6 fusion.18
  166.9 0.0 all-reduce.2.cloned.1.call-update
  166.9 2.9 convolution_convert_fusion
  169.9 470.0 %all-reduce.2.cloned.1.call-done = f32[256,768]{1,0:T(8,128)} async-done(((f32[256,768]{1,0:T(8,128)}), f32[256,768]{1,0:T(8,128)}) %all-reduce.2.cloned.1.call-update) | async-done | bytes 786448 | tf_op jit(solution)/shard_map/psum | solution.py:61
  639.9 2.1 broadcast_multiply_fusion
  (7 shorter events, 0.1 us)
Async XLA Ops:
  7.2 9.3 %copy-start = (bf16[1280,768]{1,0:T(8,128)(2,1)S(1)}, bf16[1280,768]{1,0:T(8,128)(2,1)}, u32[]{:S(2)}) copy-start(bf16[1280,768]{1,0:T(8,128)(2,1)} %param.5) | copy-start | bytes 5898244
  7.2 15.5 %all-to-all-start = ((s32[16,1,128]{2,1,0:T(1,128)}), s32[16,1,128]{2,1,0:T(1,128)S(1)}, u32[]{:S(2)}, u32[]{:S(2)}) async-start(s32[16,1,128]{2,1,0:T(1,128)} %bitcast.29), calls=%async_computation | async-start | bytes 16384 | tf_op jit(solution)/shard_map/all_to_all | solution.py:40
  31.8 5.7 copy-start.1
  31.8 17.9 %all-to-all-start.1 = ((bf16[16,128,256]{2,1,0:T(8,128)(2,1)}), bf16[16,128,256]{2,1,0:T(8,128)(2,1)}, u32[]{:S(2)}, u32[]{:S(2)}) async-start(bf16[16,128,256]{2,1,0:T(8,128)(2,1)} %bitcast.20), calls=%async_computation.1 | async-start | bytes 2097152 | tf_op jit(solution)/shard_map/all_to_all | solution.py:43
  80.8 2.5 copy-start.2
  134.4 17.3 %all-to-all-start.2 = ((bf16[16,128,256]{2,1,0:T(8,128)(2,1)}), bf16[16,128,256]{2,1,0:T(8,128)(2,1)}, u32[]{:S(2)}, u32[]{:S(2)}) async-start(bf16[16,128,256]{2,1,0:T(8,128)(2,1)} %bitcast.10), calls=%async_computation.2 | async-start | bytes 2097152 | tf_op jit(solution)/shard_map/all_to_all | solution.py:47
  140.7 499.1 %all-reduce.2.cloned.1.call-start = ((), (), s32[]{:S(2)}) async-start(), calls=%async_computation.3 | async-start | bytes 1572864 | tf_op jit(solution)/shard_map/psum | solution.py:61
Sparse Core Ops, SparseCore 0:
  167.0 472.7 all-reduce.1
where the time goes:
time: 650 us; the launch traced here: 649 us
  waiting for transfers between devices  496 us (76%)
  other arithmetic  69.2 us (11%)
  local copies, waits for them, and re-layouts  41.7 us (6%)
  starting transfers between devices  21.3 us (3%)
  between operations  14.1 us (2%)
    psum x1, waiting for transfers between devices, local(): weight_total = lax.psum(partial_value, ('group', 'dev'))  470 us
    scatter-add x1, other arithmetic, triplet_gradients(): gradient = gradient.at[triple[1]].add(-pull_term)  16.7 us
    scatter-add x1, other arithmetic, triplet_gradients(): gradient = gradient.at[triple[2]].add(push_term)  16.6 us
    scatter-add x1, other arithmetic, triplet_gradients(): gradient = gradient.at[triple[0]].add(pull_term - push_term)  15.1 us
    scatter-add x1, other arithmetic, local(): row_total = gradient[:shard_rows].at[served_index.reshape(-1)].add(return...  13.6 us
  transfers between devices with their start and end apart: 4, of which 4 were waited for; matrix products, arithmetic and copies ran while one was open for 1% of the time, Pallas kernels for 0%

commit v1 on v0

--- a/solution.py
+++ b/solution.py
@@ -58,7 +58,7 @@
         row_rounded, embeddings, (((0,), (0,)), ((), ())), preferred_element_type=jnp.float32
     )
     factor = 1.0 / math.sqrt(cotangent.shape[0] * groups * lax.axis_size("dev"))
-    weight_total = lax.psum(partial_value, ("group", "dev"))
+    weight_total = lax.psum(lax.psum(partial_value, "dev"), "group")
     return (row_grad, weight_total * factor)
 
 

time: 650 us -> 511 us (0.79)
  the two profiles are of different devices: /device:TPU:2 before, /device:TPU:32 now
where the time goes in v1:
time: 511 us; the launch traced here: 510 us
  waiting for transfers between devices  363 us (71%)
  other arithmetic  69.1 us (14%)
  local copies, waits for them, and re-layouts  41.7 us (8%)
  starting transfers between devices  16.1 us (3%)
  between operations  14.2 us (3%)
  matrix products  6.25 us (1%)
    psum x2, waiting for transfers between devices, local(): weight_total = lax.psum(lax.psum(partial_value, 'dev'), 'group')  328 us
    scatter-add x1, other arithmetic, triplet_gradients(): gradient = gradient.at[triple[1]].add(-pull_term)  16.7 us
    scatter-add x1, other arithmetic, triplet_gradients(): gradient = gradient.at[triple[2]].add(push_term)  16.6 us
    all_to_all x1, waiting for transfers between devices, local(): lax.all_to_all(served, 'group', split_axis=0, concat_axis=0, tiled=True)  15.9 us
    scatter-add x1, other arithmetic, triplet_gradients(): gradient = gradient.at[triple[0]].add(pull_term - push_term)  15.1 us
    all_to_all x1, waiting for transfers between devices, local(): lax.all_to_all(remote_grad, 'group', split_axis=0, concat_axis=0, tiled=T...  13.7 us
    scatter-add x1, other arithmetic, local(): row_total = gradient[:shard_rows].at[served_index.reshape(-1)].add(return...  13.5 us
  transfers between devices with their start and end apart: 5, of which 5 were waited for; matrix products, arithmetic and copies ran while one was open for 1% of the time, Pallas kernels for 0%

profile of v1, /device:TPU:32, one launch (start us, length us, event | category | flops | bytes accessed | tf_op | source)
XLA Modules:
  0.0 510.2 jit_solution(15778988758152788602)
XLA Ops:
  7.2 0.0 copy-start
  7.2 7.2 %all-to-all-start = ((s32[16,1,128]{2,1,0:T(1,128)}), s32[16,1,128]{2,1,0:T(1,128)S(1)}, u32[]{:S(2)}, u32[]{:S(2)}) async-start(s32[16,1,128]{2,1,0:T(1,128)} %bitcast.29), calls=%async_computation | async-start | bytes 16384 | tf_op jit(solution)/shard_map/all_to_all | solution.py:40
  14.4 0.0 copy-done
  14.4 1.7 convolution_convert_fusion.1
  16.1 5.8 %all-to-all-done = s32[16,1,128]{2,1,0:T(1,128)S(1)} async-done(((s32[16,1,128]{2,1,0:T(1,128)}), s32[16,1,128]{2,1,0:T(1,128)S(1)}, u32[]{:S(2)}, u32[]{:S(2)}) %all-to-all-start) | async-done | bytes 8224 | tf_op jit(solution)/shard_map/all_to_all | solution.py:40
  21.9 9.1 %gather_fusion = bf16[2048,256]{1,0:T(8,128)(2,1)} fusion(bf16[1280,256]{1,0:T(8,128)(2,1)S(1)} %convolution_convert_fusion.1, s32[2048]{0:T(1024)S(1)} %broadcast_clamp_fusion.3), kind=kCustom, calls=%fused_computation | custom fusion | bytes 2105344 | tf_op jit(solution)/shard_map/gather | solution.py:42
  30.9 0.0 copy-start.1
  30.9 4.5 all-to-all-start.1
  35.4 0.0 copy-done.1
  35.5 15.9 %all-to-all-done.1 = bf16[16,128,256]{2,1,0:T(8,128)(2,1)} async-done(((bf16[16,128,256]{2,1,0:T(8,128)(2,1)}), bf16[16,128,256]{2,1,0:T(8,128)(2,1)}, u32[]{:S(2)}, u32[]{:S(2)}) %all-to-all-start.1) | async-done | bytes 1048608 | tf_op jit(solution)/shard_map/all_to_all | solution.py:43
  51.4 2.5 pad_maximum_fusion
  53.9 8.3 %gather_fusion.1 = bf16[2048,256]{1,0:T(8,128)(2,1)S(1)} fusion(bf16[3328,256]{1,0:T(8,128)(2,1)} %pad_maximum_fusion, s32[2048]{0:T(1024)S(1)} %broadcast_clamp_fusion.2), kind=kCustom, calls=%fused_computation.1 | custom fusion | bytes 2105344 | tf_op jit(solution)/shard_map/gather | solution.py:13
  62.2 10.1 %gather_fusion.3 = bf16[2048,256]{1,0:T(8,128)(2,1)} fusion(bf16[3328,256]{1,0:T(8,128)(2,1)} %pad_maximum_fusion, s32[2048]{0:T(1024)S(1)} %broadcast_clamp_fusion), kind=kCustom, calls=%fused_computation.3 | custom fusion | bytes 2105344 | tf_op jit(solution)/shard_map/gather | solution.py:15
  72.4 10.1 %gather_fusion.2 = bf16[2048,256]{1,0:T(8,128)(2,1)} fusion(bf16[3328,256]{1,0:T(8,128)(2,1)} %pad_maximum_fusion, s32[2048]{0:T(1024)S(1)} %broadcast_clamp_fusion.1), kind=kCustom, calls=%fused_computation.2 | custom fusion | bytes 2105344 | tf_op jit(solution)/shard_map/gather | solution.py:14
  82.4 0.0 copy-start.2
  82.5 2.5 multiply_reduce_fusion.1
  85.0 0.0 copy-done.2
  85.0 15.1 %scatter_custom_fusion = f32[3328,256]{1,0:T(8,128)} fusion(s32[2048]{0:T(1024)S(1)} %bitcast.28, bf16[2048,256]{1,0:T(8,128)(2,1)} %gather_fusion.3, bf16[2048,256]{1,0:T(8,128)(2,1)S(1)} %gather_fusion.1, bf16[2048,256]{1,0:T(8,128)(2,1)} %gather_fusion.2, f32[]{:T(128)} %constant.8.clone.1, f32[2048]{0:T(1024)S(1)} %get-tuple-element.8, ...), kind=kCustom, calls=%fused_computation.17 | custom fusion | flops 4718592 | bytes 6569988 | tf_op jit(solution)/shard_map/scatter-add | solution.py:26
  100.1 16.7 %scatter_custom_fusion.1 = f32[3328,256]{1,0:T(8,128)} fusion(f32[3328,256]{1,0:T(8,128)} %scatter_custom_fusion, s32[2048]{0:T(1024)S(1)} %bitcast.26, bf16[2048,256]{1,0:T(8,128)(2,1)} %gather_fusion.2, bf16[2048,256]{1,0:T(8,128)(2,1)S(1)} %gather_fusion.1, f32[2048]{0:T(1024)S(1)} %get-tuple-element.7), kind=kCustom, calls=%fused_computation.15 | custom fusion | flops 3145728 | bytes 5513216 | tf_op jit(solution)/shard_map/scatter-add | solution.py:27
  116.8 16.6 %scatter_custom_fusion.2 = f32[3328,256]{1,0:T(8,128)} fusion(f32[3328,256]{1,0:T(8,128)} %scatter_custom_fusion.1, s32[2048]{0:T(1024)S(1)} %bitcast.24, bf16[2048,256]{1,0:T(8,128)(2,1)} %gather_fusion.3, bf16[2048,256]{1,0:T(8,128)(2,1)S(1)} %gather_fusion.1, f32[2048]{0:T(1024)S(1)} %get-tuple-element.8), kind=kCustom, calls=%fused_computation.23 | custom fusion | flops 2621440 | bytes 5513216 | tf_op jit(solution)/shard_map/scatter-add | solution.py:28
  133.4 2.7 slice.38
  136.1 4.3 all-to-all-start.2
  140.4 0.0 all-reduce.3.cloned.1.call-start
  140.5 1.4 slice.32
  141.9 13.7 %all-to-all-done.2 = bf16[16,128,256]{2,1,0:T(8,128)(2,1)} async-done(((bf16[16,128,256]{2,1,0:T(8,128)(2,1)}), bf16[16,128,256]{2,1,0:T(8,128)(2,1)}, u32[]{:S(2)}, u32[]{:S(2)}) %all-to-all-start.2) | async-done | bytes 1048608 | tf_op jit(solution)/shard_map/all_to_all | solution.py:47
  155.6 13.5 %scatter_custom_fusion.3 = f32[1280,256]{1,0:T(8,128)S(1)} fusion(f32[1280,256]{1,0:T(8,128)S(1)} %slice.32, s32[2048]{0:T(1024)S(1)} %bitcast.22, bf16[2048,256]{1,0:T(8,128)(2,1)} %bitcast.12), kind=kCustom, calls=%fused_computation.13 | custom fusion | flops 1048576 | bytes 2359296 | tf_op jit(solution)/shard_map/scatter-add | solution.py:51
  169.1 1.6 fusion.18
  170.7 0.0 all-reduce.3.cloned.1.call-update
  170.7 0.0 all-reduce.5.cloned.1.call-start
  170.8 208.0 %all-reduce.3.cloned.1.call-done = f32[256,768]{1,0:T(8,128)} async-done(((f32[256,768]{1,0:T(8,128)}), f32[256,768]{1,0:T(8,128)}) %all-reduce.3.cloned.1.call-update) | async-done | bytes 786448 | tf_op jit(solution)/shard_map/psum | solution.py:61
  378.8 0.0 all-reduce.5.cloned.1.call-update
  378.8 3.0 convolution_convert_fusion
  381.7 119.6 %all-reduce.5.cloned.1.call-done = f32[256,768]{1,0:T(8,128)} async-done(((f32[256,768]{1,0:T(8,128)}), f32[256,768]{1,0:T(8,128)}) %all-reduce.5.cloned.1.call-update) | async-done | bytes 786448 | tf_op jit(solution)/shard_map/psum | solution.py:61
  501.3 2.1 broadcast_multiply_fusion
  (7 shorter events, 0.1 us)
Async XLA Ops:
  7.2 7.2 %copy-start = (bf16[1280,768]{1,0:T(8,128)(2,1)S(1)}, bf16[1280,768]{1,0:T(8,128)(2,1)}, u32[]{:S(2)}) copy-start(bf16[1280,768]{1,0:T(8,128)(2,1)} %param.5) | copy-start | bytes 5898244
  7.2 14.7 %all-to-all-start = ((s32[16,1,128]{2,1,0:T(1,128)}), s32[16,1,128]{2,1,0:T(1,128)S(1)}, u32[]{:S(2)}, u32[]{:S(2)}) async-start(s32[16,1,128]{2,1,0:T(1,128)} %bitcast.29), calls=%async_computation | async-start | bytes 16384 | tf_op jit(solution)/shard_map/all_to_all | solution.py:40
  30.9 4.5 copy-start.1
  30.9 20.4 %all-to-all-start.1 = ((bf16[16,128,256]{2,1,0:T(8,128)(2,1)}), bf16[16,128,256]{2,1,0:T(8,128)(2,1)}, u32[]{:S(2)}, u32[]{:S(2)}) async-start(bf16[16,128,256]{2,1,0:T(8,128)(2,1)} %bitcast.20), calls=%async_computation.1 | async-start | bytes 2097152 | tf_op jit(solution)/shard_map/all_to_all | solution.py:43
  82.4 2.5 copy-start.2
  136.1 19.5 %all-to-all-start.2 = ((bf16[16,128,256]{2,1,0:T(8,128)(2,1)}), bf16[16,128,256]{2,1,0:T(8,128)(2,1)}, u32[]{:S(2)}, u32[]{:S(2)}) async-start(bf16[16,128,256]{2,1,0:T(8,128)(2,1)} %bitcast.10), calls=%async_computation.2 | async-start | bytes 2097152 | tf_op jit(solution)/shard_map/all_to_all | solution.py:47
  140.4 238.3 %all-reduce.3.cloned.1.call-start = ((), (), s32[]{:S(2)}) async-start(), calls=%async_computation.3 | async-start | bytes 1572864 | tf_op jit(solution)/shard_map/psum | solution.py:61
  170.7 330.6 %all-reduce.5.cloned.1.call-start = ((), (), s32[]{:S(2)}) async-start(), calls=%async_computation.4 | async-start | bytes 1572864 | tf_op jit(solution)/shard_map/psum | solution.py:61
Sparse Core Ops, SparseCore 0:
  170.8 207.8 all-reduce.2
  382.3 118.9 all-reduce.4
